TPU v7x, 512 devices: a whole 4x8x8 slice. The times are simulated.
512 devices in a mesh: seq: 64 (over z, x, core), head: 8 (over y).
Axes of the slice: x: 4, y: 8, z: 8, core: 2. Of those that a mesh axis runs over, the one named last changes fastest.
Arguments:
- query_states: bfloat16 [16384, 4096], P(('seq', 'head')), may hold values from -8 to 8
- key_states: bfloat16 [16384, 4096], P(('seq', 'head')), may hold values from -8 to 8
- value_states: bfloat16 [16384, 4096], P(('seq', 'head')), may hold values from -8 to 8
- out_grad: bfloat16 [16384, 4096], P(('seq', 'head')), may hold values from -6 to 6
Outputs:
- attended: bfloat16 [16384, 4096], P('seq', 'head')
- query_grad: bfloat16 [16384, 4096], P('seq', 'head')
- key_grad: bfloat16 [16384, 4096], P('seq', 'head')
- value_grad: bfloat16 [16384, 4096], P('seq', 'head')
All inputs are finite; a program needn't handle non-finite values.
Results may differ from a plain program's by a relative error of at most 0.025.
Values may be sent and summed in bfloat16 or wider, within the bound.
A program may use at most 64 MiB of HBM per device.

v0:
```python
import jax
import jax.numpy as jnp
from jax import lax
from jax.sharding import PartitionSpec as P

HEAD_DIM = 128
BLOCK = 128
MASKED = -1e30


def broadcast(block, axis, owner):
    block = jnp.where(lax.axis_index(axis) == owner, block, jnp.zeros_like(block))
    return lax.psum(block, axis)


def with_halo(cells, sides, width):
    for axis, dim in sides:
        count = lax.axis_size(axis)
        ends = count - 1
        head = lax.slice_in_dim(cells, 0, width, axis=dim)
        tail = lax.slice_in_dim(cells, cells.shape[dim] - width, cells.shape[dim], axis=dim)
        cells = jnp.concatenate(
            [
                lax.ppermute(tail, axis, [(i, (i + 1) % count) for i in range(ends)]),
                cells,
                lax.ppermute(head, axis, [((i + 1) % count, i) for i in range(ends)]),
            ],
            axis=dim,
        )
    return cells


def shifted(value, axis, steps):
    count = lax.axis_size(axis)
    leading, last = (max(0, -steps), min(count, count - steps))
    return lax.ppermute(value, axis, [(source, source + steps) for source in range(leading, last)])


def local(query_states, key_states, value_states, out_grad):
    query_states, key_states, value_states, out_grad = (
        lax.all_to_all(query_states, "head", split_axis=1, concat_axis=0, tiled=True),
        lax.all_to_all(key_states, "head", split_axis=1, concat_axis=0, tiled=True),
        lax.all_to_all(value_states, "head", split_axis=1, concat_axis=0, tiled=True),
        lax.all_to_all(out_grad, "head", split_axis=1, concat_axis=0, tiled=True),
    )
    local_rows = query_states.shape[0]
    head_count = query_states.shape[1] // HEAD_DIM
    block_count = local_rows // BLOCK
    position = lax.axis_index("seq")
    total_blocks = block_count * lax.axis_size("seq")
    inverse_square_root = HEAD_DIM ** (-0.5)

    def as_blocks(array):
        return array.reshape(block_count, BLOCK, head_count, HEAD_DIM)

    def as_heads(array):
        return array.reshape(array.shape[0], head_count, HEAD_DIM)

    leading = jnp.stack(
        [query_states[:BLOCK], key_states[:BLOCK], value_states[:BLOCK], out_grad[:BLOCK]]
    )
    leading = broadcast(leading, "seq", 0)
    glob_query = as_heads(leading[0])
    glob_key = as_heads(leading[1])
    glob_value = as_heads(leading[2])
    glob_grad = as_heads(leading[3])
    extended = with_halo(jnp.stack([key_states, value_states]), (("seq", 1),), BLOCK)

    def windows(rows_ext, shared):
        spread = jnp.broadcast_to(shared[None], (block_count, BLOCK, head_count, HEAD_DIM))
        return jnp.concatenate(
            [
                spread,
                as_blocks(rows_ext[:local_rows]),
                as_blocks(rows_ext[BLOCK : BLOCK + local_rows]),
                as_blocks(rows_ext[2 * BLOCK :]),
            ],
            1,
        )

    window_key_rows = windows(extended[0], glob_key)
    window_value_rows = windows(extended[1], glob_value)
    block_ids = position * block_count + jnp.arange(block_count)
    allowed = jnp.stack(
        [block_ids >= 2, block_ids >= 1, block_ids >= 0, block_ids + 1 < total_blocks], 1
    )
    allowed = jnp.repeat(allowed, BLOCK, axis=1)[:, None, None, :]
    live_rows = (block_ids != 0)[:, None, None, None]
    query_blocks = as_blocks(query_states)
    grad_blocks = as_blocks(out_grad)
    logit_scores = (
        jnp.einsum(
            "cqhd,ckhd->chqk", query_blocks, window_key_rows, preferred_element_type=jnp.float32
        )
        * inverse_square_root
    )
    logit_scores = jnp.where(allowed, logit_scores, MASKED)
    row_top = jnp.max(logit_scores, -1, keepdims=True)
    log_total = row_top + jnp.log(jnp.sum(jnp.exp(logit_scores - row_top), -1, keepdims=True))
    weights = jnp.where(allowed & live_rows, jnp.exp(logit_scores - log_total), 0.0)
    probabilities = weights.astype(jnp.bfloat16)
    window_output = jnp.einsum(
        "chqk,ckhd->cqhd", probabilities, window_value_rows, preferred_element_type=jnp.float32
    ).astype(jnp.bfloat16)
    local_keys = as_heads(key_states)
    local_values = as_heads(value_states)
    glob_scores = (
        jnp.einsum("qhd,khd->hqk", glob_query, local_keys, preferred_element_type=jnp.float32)
        * inverse_square_root
    )
    local_top = jnp.max(glob_scores, -1)
    glob_top = lax.pmax(local_top, "seq")
    glob_total = lax.psum(jnp.sum(jnp.exp(glob_scores - glob_top[:, :, None]), -1), "seq")
    glob_log = glob_top + jnp.log(glob_total)
    glob_weights = jnp.exp(glob_scores - glob_log[:, :, None])
    glob_probs = glob_weights.astype(jnp.bfloat16)
    glob_part = jnp.einsum(
        "hqk,khd->qhd", glob_probs, local_values, preferred_element_type=jnp.float32
    )
    glob_out = lax.psum(glob_part, "seq").astype(jnp.bfloat16)
    glob_delta = jnp.sum(glob_grad.astype(jnp.float32) * glob_out.astype(jnp.float32), -1)
    glob_dprob = jnp.einsum(
        "qhd,khd->hqk", glob_grad, local_values, preferred_element_type=jnp.float32
    )
    glob_dscore = (glob_weights * (glob_dprob - glob_delta.T[:, :, None])).astype(jnp.bfloat16)
    glob_dquery_part = (
        jnp.einsum("hqk,khd->qhd", glob_dscore, local_keys, preferred_element_type=jnp.float32)
        * inverse_square_root
    )
    key_from_glob = (
        jnp.einsum("hqk,qhd->khd", glob_dscore, glob_query, preferred_element_type=jnp.float32)
        * inverse_square_root
    )
    value_from_glob = jnp.einsum(
        "hqk,qhd->khd", glob_probs, glob_grad, preferred_element_type=jnp.float32
    )
    band_delta = jnp.sum(
        grad_blocks.astype(jnp.float32) * window_output.astype(jnp.float32), -1
    ).transpose(0, 2, 1)
    probability_gradient = jnp.einsum(
        "cqhd,ckhd->chqk", grad_blocks, window_value_rows, preferred_element_type=jnp.float32
    )
    score_gradient = (weights * (probability_gradient - band_delta[:, :, :, None])).astype(
        jnp.bfloat16
    )
    window_query_gradient = (
        jnp.einsum(
            "chqk,ckhd->cqhd", score_gradient, window_key_rows, preferred_element_type=jnp.float32
        )
        * inverse_square_root
    )
    window_key_gradient = (
        jnp.einsum(
            "chqk,cqhd->ckhd", score_gradient, query_blocks, preferred_element_type=jnp.float32
        )
        * inverse_square_root
    )
    window_value_gradient = jnp.einsum(
        "chqk,cqhd->ckhd", probabilities, grad_blocks, preferred_element_type=jnp.float32
    )
    stacked = jnp.stack([window_key_gradient, window_value_gradient]).reshape(
        2, block_count, 4, BLOCK, head_count, HEAD_DIM
    )
    glob_piece = jnp.sum(stacked[:, :, 0], 1)
    before = stacked[:, :, 1]
    middle = stacked[:, :, 2]
    after = stacked[:, :, 3]
    empty_block = jnp.zeros((2, 1, BLOCK, head_count, HEAD_DIM), jnp.float32)
    inner = (
        middle
        + jnp.concatenate([before[:, 1:], empty_block], 1)
        + jnp.concatenate([empty_block, after[:, :-1]], 1)
    )
    from_right = shifted(before[:, 0].astype(jnp.bfloat16), "seq", -1).astype(jnp.float32)
    from_left = shifted(after[:, -1].astype(jnp.bfloat16), "seq", 1).astype(jnp.float32)
    inner = inner.at[:, 0].add(from_left)
    inner = inner.at[:, -1].add(from_right)
    glob_dquery, glob_dkey, glob_dvalue = lax.psum(
        (glob_dquery_part, glob_piece[0], glob_piece[1]), "seq"
    )
    local_grads = inner.reshape(2, local_rows, head_count, HEAD_DIM) + jnp.stack(
        [key_from_glob, value_from_glob]
    )
    is_first = ((jnp.arange(local_rows) < BLOCK) & (position == 0))[:, None, None]

    def padded(array):
        return jnp.concatenate(
            [array, jnp.zeros((local_rows - BLOCK,) + array.shape[1:], array.dtype)], 0
        )

    key_grad = local_grads[0] + jnp.where(is_first, padded(glob_dkey), 0.0)
    value_grad = local_grads[1] + jnp.where(is_first, padded(glob_dvalue), 0.0)
    query_grad = jnp.where(
        is_first,
        padded(glob_dquery),
        window_query_gradient.reshape(local_rows, head_count, HEAD_DIM),
    )
    attended = jnp.where(
        is_first, padded(glob_out), window_output.reshape(local_rows, head_count, HEAD_DIM)
    )
    return (
        attended.reshape(local_rows, -1),
        query_grad.reshape(local_rows, -1).astype(jnp.bfloat16),
        key_grad.reshape(local_rows, -1).astype(jnp.bfloat16),
        value_grad.reshape(local_rows, -1).astype(jnp.bfloat16),
    )


def solution(mesh):
    return jax.shard_map(
        local,
        mesh=mesh,
        in_specs=(
            P(("seq", "head"), None),
            P(("seq", "head"), None),
            P(("seq", "head"), None),
            P(("seq", "head"), None),
        ),
        out_specs=(P("seq", "head"), P("seq", "head"), P("seq", "head"), P("seq", "head")),
        check_vma=False,
    )
```

profile of v0, /device:TPU:2, one launch (start us, length us, event | category | flops | bytes accessed | tf_op | source)
XLA Modules:
  0.0 1251.9 jit_solution(274508605988238875)
XLA Ops:
  8.9 7.1 all-to-all-start
  17.7 10.2 all-to-all-done
  27.9 3.4 all-to-all-start.1
  32.1 9.7 all-to-all-done.1
  41.7 3.4 all-to-all-start.2
  45.9 9.6 all-to-all-done.2
  55.5 3.4 all-to-all-start.3
  59.2 10.1 all-to-all-done.3
  70.4 1.9 collective-permute-start
  72.4 3.6 collective-permute-start.1
  78.0 184.9 %all-reduce.12.cloned.1.call-done = bf16[4,128,512]{2,1,0:T(8,128)(2,1)} async-done(((bf16[4,128,512]{2,1,0:T(8,128)(2,1)}), bf16[4,128,512]{2,1,0:T(8,128)(2,1)}) %all-reduce.12.cloned.1.call-update) | async-done | bytes 524304 | tf_op jit(solution)/shard_map/psum | solution.py:13
  276.4 1.9 copy.144
  278.4 2.9 copy.143
  281.3 2.4 fusion.20
  287.5 120.4 %pmax.7 = f32[4,128]{1,0:T(4,128)S(1)} all-reduce(f32[4,128]{1,0:T(4,128)S(1)} %get-tuple-element.71), channel_id=1, replica_groups=mesh['seq'=64,'head'=8] {'seq'}, use_global_device_ids=true, to_apply=%region_2.3 | all-reduce | flops 512 | bytes 4096 | tf_op jit(solution)/shard_map/pmax | solution.py:112
  408.2 124.1 %psum.43 = f32[4,128]{1,0:T(4,128)S(1)} all-reduce(f32[4,128]{1,0:T(4,128)S(1)} %exponential_reduce_fusion), channel_id=1, replica_groups=mesh['seq'=64,'head'=8] {'seq'}, use_global_device_ids=true, to_apply=%region_4.5 | all-reduce | flops 512 | bytes 4096 | tf_op jit(solution)/shard_map/psum | solution.py:113
  533.3 246.8 %all-reduce.15 = bf16[128,4,128]{0,2,1:T(8,128)(2,1)S(1)} all-reduce(f32[128,4,128]{0,2,1:T(8,128)} %convolution_bitcast_fusion.1), channel_id=1, replica_groups=mesh['seq'=64,'head'=8] {'seq'}, use_global_device_ids=true, to_apply=%region_5.6 | all-reduce | flops 65536 | bytes 393216 | tf_op jit(solution)/shard_map/psum | solution.py:120
  781.8 246.2 %all-reduce.16 = bf16[128,4,128]{0,2,1:T(8,128)(2,1)S(1)} all-reduce(f32[128,4,128]{0,2,1:T(8,128)S(1)} %fusion.10), channel_id=1, replica_groups=mesh['seq'=64,'head'=8] {'seq'}, use_global_device_ids=true, to_apply=%region_9.10 | all-reduce | flops 65536 | bytes 393216 | tf_op jit(solution)/shard_map/psum | solution.py:178
  1033.1 1.9 copy.148
  1035.8 1.9 slice_bitcast_fusion.2
  1037.7 1.9 collective-permute-start.2
  1039.6 3.8 collective-permute-start.3
  1048.4 12.0 scatter-add.9
  1061.4 180.8 %all-reduce.14.cloned.1.call-done = (f32[128,4,128]{0,2,1:T(8,128)}, f32[128,4,128]{0,2,1:T(8,128)}) async-done(((f32[128,4,128]{0,2,1:T(8,128)}, f32[128,4,128]{0,2,1:T(8,128)}), (f32[128,4,128]{0,2,1:T(8,128)}, f32[128,4,128]{0,2,1:T(8,128)})) %all-reduce.14.cloned.1.call-update) | async-done | bytes 524304 | tf_op jit(solution)/shard_map/psum | solution.py:178
  (124 shorter events, 42.9 us)
Async XLA Ops:
  7.2 24.2 %copy-start.9 = (bf16[32,4096]{1,0:T(8,128)(2,1)S(1)}, bf16[32,4096]{1,0:T(8,128)(2,1)}, u32[]{:S(2)}) copy-start(bf16[32,4096]{1,0:T(8,128)(2,1)} %param.10) | copy-start | bytes 786436
  7.2 38.0 %copy-start.10 = (bf16[32,4096]{1,0:T(8,128)(2,1)S(1)}, bf16[32,4096]{1,0:T(8,128)(2,1)}, u32[]{:S(2)}) copy-start(bf16[32,4096]{1,0:T(8,128)(2,1)} %param.11) | copy-start | bytes 786436
  8.9 19.0 %all-to-all-start = ((bf16[32,8,512]{2,0,1:T(8,128)(2,1)}), bf16[32,8,512]{2,0,1:T(8,128)(2,1)S(1)}, u32[]{:S(2)}, u32[]{:S(2)}) async-start(bf16[32,8,512]{2,0,1:T(8,128)(2,1)} %bitcast.136), calls=%async_computation | async-start | bytes 524288 | tf_op jit(solution)/shard_map/all_to_all | solution.py:41
  27.9 13.8 %all-to-all-start.1 = ((bf16[32,8,512]{2,0,1:T(8,128)(2,1)}), bf16[32,8,512]{2,0,1:T(8,128)(2,1)S(1)}, u32[]{:S(2)}, u32[]{:S(2)}) async-start(bf16[32,8,512]{2,0,1:T(8,128)(2,1)} %bitcast.135), calls=%async_computation.1 | async-start | bytes 524288 | tf_op jit(solution)/shard_map/all_to_all | solution.py:42
  41.7 13.8 %all-to-all-start.2 = ((bf16[32,8,512]{2,0,1:T(8,128)(2,1)}), bf16[32,8,512]{2,0,1:T(8,128)(2,1)S(1)}, u32[]{:S(2)}, u32[]{:S(2)}) async-start(bf16[32,8,512]{2,0,1:T(8,128)(2,1)} %bitcast.134), calls=%async_computation.2 | async-start | bytes 524288 | tf_op jit(solution)/shard_map/all_to_all | solution.py:43
  55.5 13.8 %all-to-all-start.3 = ((bf16[32,8,512]{2,0,1:T(8,128)(2,1)}), bf16[32,8,512]{2,0,1:T(8,128)(2,1)S(1)}, u32[]{:S(2)}, u32[]{:S(2)}) async-start(bf16[32,8,512]{2,0,1:T(8,128)(2,1)} %bitcast.133), calls=%async_computation.3 | async-start | bytes 524288 | tf_op jit(solution)/shard_map/all_to_all | solution.py:44
  58.9 203.9 %all-reduce.12.cloned.1.call-start = ((), (), s32[]{:S(2)}) async-start(), calls=%async_computation.4 | async-start | bytes 1048576 | tf_op jit(solution)/shard_map/psum | solution.py:13
  70.3 1171.9 %all-reduce.14.cloned.1.call-start = ((), (), s32[]{:S(2)}) async-start(), calls=%async_computation.5 | async-start | bytes 1048576 | tf_op jit(solution)/shard_map/psum | solution.py:178
  70.4 194.4 %collective-permute-start = (bf16[2,128,512]{2,1,0:T(8,128)(2,1)S(1)}, bf16[2,128,512]{2,1,0:T(8,128)(2,1)}, u32[]{:S(2)}, u32[]{:S(2)}) collective-permute-start(bf16[2,128,512]{2,1,0:T(8,128)(2,1)S(1)} %get-tuple-element.63), channel_id=1, source_target_pairs={{0,8},{8,16},{16,24},{24,32},{32,40},{40,48},{48,56},{56,64},{64,7... | collective-permute-start | bytes 786440 | tf_op jit(solution)/shard_map/ppermute | solution.py:24
  72.4 192.4 %collective-permute-start.1 = (bf16[2,128,512]{2,1,0:T(8,128)(2,1)S(1)}, bf16[2,128,512]{2,1,0:T(8,128)(2,1)}, u32[]{:S(2)}, u32[]{:S(2)}) collective-permute-start(bf16[2,128,512]{2,1,0:T(8,128)(2,1)S(1)} %get-tuple-element.64), channel_id=1, source_target_pairs={{8,0},{16,8},{24,16},{32,24},{40,32},{48,40},{56,48},{64,56},{72,6... | collective-permute-start | bytes 786440 | tf_op jit(solution)/shard_map/ppermute | solution.py:26
  266.3 3.7 copy-start.15
  266.4 3.6 copy-start.16
  268.1 1.9 copy-start.12
  271.7 1.8 copy-start.14
  283.7 3.1 copy-start.8
  283.7 3.3 copy-start.7
  287.1 494.1 %copy-start.3 = (bf16[1,128,512]{1,2,0:T(8,128)(2,1)}, bf16[1,128,512]{1,2,0:T(8,128)(2,1)S(1)}, u32[]{:S(2)}) copy-start(bf16[1,128,512]{1,2,0:T(8,128)(2,1)S(1)} %copy.116) | copy-start | bytes 393220
  781.5 249.8 %copy-start.6 = (bf16[128,4,128]{0,2,1:T(8,128)(2,1)S(1)}, bf16[128,4,128]{0,2,1:T(8,128)(2,1)}, u32[]{:S(2)}) copy-start(bf16[128,4,128]{0,2,1:T(8,128)(2,1)} %copy-done.5) | copy-start | bytes 393220
  1031.3 12.1 copy-start.4
  1033.1 11.4 copy-start
  1037.7 8.1 collective-permute-start.2
  1039.6 8.2 collective-permute-start.3
  1047.8 13.5 %copy-start.1 = (f32[1,256,4,128]{1,3,2,0:T(8,128)S(1)}, f32[1,256,4,128]{1,3,2,0:T(8,128)}, u32[]{:S(2)}) copy-start(f32[1,256,4,128]{1,3,2,0:T(8,128)} %fusion.7) | copy-start | bytes 1572868
  1047.8 13.5 %copy-start.2 = (f32[1,256,4,128]{1,3,2,0:T(8,128)S(1)}, f32[1,256,4,128]{1,3,2,0:T(8,128)}, u32[]{:S(2)}) copy-start(f32[1,256,4,128]{1,3,2,0:T(8,128)} %convolution_bitcast_fusion) | copy-start | bytes 1572868
  (3 other events, 3.8 us)
Sparse Core Ops, SparseCore 0:
  70.4 192.3 all-reduce.11
  1043.5 198.6 all-reduce.13
where the time goes:
time: 1250 us
  blocking collectives  737 us (59%)
  waiting for transfers between devices  405 us (32%)
  local copies, waits for them, and re-layouts  41.3 us (3%)
  starting transfers between devices  28.7 us (2%)
  between operations  14.7 us (1%)
  matrix products  13.1 us (1%)
    psum x1, blocking collectives, local(): glob_out = lax.psum(glob_part, 'seq').astype(jnp.bfloat16)  247 us
    psum x1, blocking collectives, local(): lax.psum((glob_dquery_part, glob_piece[0], glob_piece[1]), 'seq')  246 us
    psum x1, waiting for transfers between devices, broadcast(): return lax.psum(block, axis)  185 us
    psum x1, waiting for transfers between devices, local(): lax.psum((glob_dquery_part, glob_piece[0], glob_piece[1]), 'seq')  181 us
    psum x1, blocking collectives, local(): lax.psum(jnp.sum(jnp.exp(glob_scores - glob_top[:, :, None]), -1), 'seq')  124 us
    pmax x1, blocking collectives, local(): glob_top = lax.pmax(local_top, 'seq')  120 us
  transfers between devices with their start and end apart: 10, of which 6 were waited for; matrix products, arithmetic and copies ran while one was open for 2% of the time, Pallas kernels for 0%

commit v1 on v0

--- a/solution.py
+++ b/solution.py
@@ -117,7 +117,7 @@
     glob_part = jnp.einsum(
         "hqk,khd->qhd", glob_probs, local_values, preferred_element_type=jnp.float32
     )
-    glob_out = lax.psum(glob_part, "seq").astype(jnp.bfloat16)
+    glob_out = jnp.sum(lax.all_gather(glob_part, "seq"), axis=0).astype(jnp.bfloat16)
     glob_delta = jnp.sum(glob_grad.astype(jnp.float32) * glob_out.astype(jnp.float32), -1)
     glob_dprob = jnp.einsum(
         "qhd,khd->hqk", glob_grad, local_values, preferred_element_type=jnp.float32

time: 1250 us -> 888 us (0.71)
  the two profiles are of different devices: /device:TPU:2 before, /device:TPU:8 now
where the time goes in v1:
time: 888 us; the launch traced here: 887 us
  blocking collectives  497 us (56%)
  waiting for transfers between devices  268 us (30%)
  local copies, waits for them, and re-layouts  41.7 us (5%)
  starting transfers between devices  34.9 us (4%)
  other arithmetic  18.2 us (2%)
  between operations  14.4 us (2%)
  matrix products  12.9 us (1%)
    psum x1, blocking collectives, local(): lax.psum((glob_dquery_part, glob_piece[0], glob_piece[1]), 'seq')  248 us
    psum x1, waiting for transfers between devices, broadcast(): return lax.psum(block, axis)  193 us
    pmax x1, blocking collectives, local(): glob_top = lax.pmax(local_top, 'seq')  125 us
    psum x1, blocking collectives, local(): lax.psum(jnp.sum(jnp.exp(glob_scores - glob_top[:, :, None]), -1), 'seq')  124 us
    all_gather x1, waiting for transfers between devices, local(): lax.all_gather(glob_part, 'seq')  42.2 us
  transfers between devices with their start and end apart: 11, of which 6 were waited for; matrix products, arithmetic and copies ran while one was open for 7% of the time, Pallas kernels for 0%

profile of v1, /device:TPU:8, one launch (start us, length us, event | category | flops | bytes accessed | tf_op | source)
XLA Modules:
  0.0 886.9 jit_solution(13911110328676126059)
XLA Ops:
  7.2 1.7 copy.189
  8.9 9.1 %all-to-all-start = ((bf16[32,8,512]{2,0,1:T(8,128)(2,1)}), bf16[32,8,512]{2,0,1:T(8,128)(2,1)S(1)}, u32[]{:S(2)}, u32[]{:S(2)}) async-start(bf16[32,8,512]{2,0,1:T(8,128)(2,1)} %bitcast.137), calls=%async_computation | async-start | bytes 524288 | tf_op jit(solution)/shard_map/all_to_all | solution.py:41
  18.1 1.7 copy.188
  19.7 7.4 all-to-all-done
  27.1 4.8 all-to-all-start.1
  32.6 8.0 all-to-all-done.1
  40.6 5.1 all-to-all-start.2
  46.4 7.9 all-to-all-done.2
  54.3 5.2 all-to-all-start.3
  59.5 9.0 %all-to-all-done.3 = bf16[32,8,512]{2,0,1:T(8,128)(2,1)S(1)} async-done(((bf16[32,8,512]{2,0,1:T(8,128)(2,1)}), bf16[32,8,512]{2,0,1:T(8,128)(2,1)S(1)}, u32[]{:S(2)}, u32[]{:S(2)}) %all-to-all-start.3) | async-done | bytes 262176 | tf_op jit(solution)/shard_map/all_to_all | solution.py:44
  69.7 193.4 %all-reduce.11.cloned.1.call-done = bf16[4,128,512]{2,1,0:T(8,128)(2,1)} async-done(((bf16[4,128,512]{2,1,0:T(8,128)(2,1)}), bf16[4,128,512]{2,1,0:T(8,128)(2,1)}) %all-reduce.11.cloned.1.call-update) | async-done | bytes 524304 | tf_op jit(solution)/shard_map/psum | solution.py:13
  264.6 125.2 %pmax.7 = f32[4,128]{1,0:T(4,128)S(1)} all-reduce(f32[4,128]{1,0:T(4,128)S(1)} %get-tuple-element.71), channel_id=1, replica_groups=mesh['seq'=64,'head'=8] {'seq'}, use_global_device_ids=true, to_apply=%region_2.3 | all-reduce | flops 512 | bytes 4096 | tf_op jit(solution)/shard_map/pmax | solution.py:112
  390.1 124.1 %psum.36 = f32[4,128]{1,0:T(4,128)S(1)} all-reduce(f32[4,128]{1,0:T(4,128)S(1)} %exponential_reduce_fusion), channel_id=1, replica_groups=mesh['seq'=64,'head'=8] {'seq'}, use_global_device_ids=true, to_apply=%region_4.5 | all-reduce | flops 512 | bytes 4096 | tf_op jit(solution)/shard_map/psum | solution.py:113
  516.2 2.5 collective-permute-start
  527.6 1.8 fusion.36
  529.4 2.0 copy.141
  531.5 3.4 multiply_reduce_fusion
  536.8 1.7 convolution_multiply_fusion
  538.5 2.9 copy.140
  543.9 5.4 collective-permute-start.2
  563.4 12.0 %scatter-add.9 = f32[2,2,128,4,128]{2,1,4,3,0:T(2,128)S(1)} dynamic-update-slice(f32[2,2,128,4,128]{2,1,4,3,0:T(2,128)S(1)} %copy.143, f32[2,1,128,4,128]{2,1,4,3,0:T(1,128)S(1)} %add.115, s32[]{:T(128)} %constant.80.clone.1, s32[]{:T(128)} %constant.86.clone.1, s32[]{:T(128)} %constant.80.clone.1, s32[]{:T(128)} %constant.80.clone.1, s32[]{:T(128)} %constant.80.clone.1) | dynamic-update-slice | bytes 1048580 | tf_op jit(solution)/shard_map/scatter-add | solution.py:177
  576.3 42.2 %all-gather.3.cloned.1.call-done = f32[8192,4,128]{2,0,1:T(8,128)} async-done(((f32[128,4,128]{2,0,1:T(8,128)}), f32[8192,4,128]{2,0,1:T(8,128)}) %all-gather.3.cloned.1.call-update) | async-done | bytes 16777232 | tf_op jit(solution)/shard_map/all_gather | solution.py:120
  618.5 6.7 reduce_sum.55
  626.8 247.7 %all-reduce.14 = bf16[128,4,128]{0,2,1:T(8,128)(2,1)S(1)} all-reduce(f32[128,4,128]{0,2,1:T(8,128)S(1)} %fusion.10), channel_id=1, replica_groups=mesh['seq'=64,'head'=8] {'seq'}, use_global_device_ids=true, to_apply=%region_9.10 | all-reduce | flops 65536 | bytes 393216 | tf_op jit(solution)/shard_map/psum | solution.py:178
  (154 shorter events, 41.7 us)
Async XLA Ops:
  7.2 24.7 %copy-start.18 = (bf16[32,4096]{1,0:T(8,128)(2,1)S(1)}, bf16[32,4096]{1,0:T(8,128)(2,1)}, u32[]{:S(2)}) copy-start(bf16[32,4096]{1,0:T(8,128)(2,1)} %param.10) | copy-start | bytes 786436
  7.2 38.5 %copy-start.19 = (bf16[32,4096]{1,0:T(8,128)(2,1)S(1)}, bf16[32,4096]{1,0:T(8,128)(2,1)}, u32[]{:S(2)}) copy-start(bf16[32,4096]{1,0:T(8,128)(2,1)} %param.11) | copy-start | bytes 786436
  8.9 18.2 %all-to-all-start = ((bf16[32,8,512]{2,0,1:T(8,128)(2,1)}), bf16[32,8,512]{2,0,1:T(8,128)(2,1)S(1)}, u32[]{:S(2)}, u32[]{:S(2)}) async-start(bf16[32,8,512]{2,0,1:T(8,128)(2,1)} %bitcast.137), calls=%async_computation | async-start | bytes 524288 | tf_op jit(solution)/shard_map/all_to_all | solution.py:41
  27.1 13.5 %all-to-all-start.1 = ((bf16[32,8,512]{2,0,1:T(8,128)(2,1)}), bf16[32,8,512]{2,0,1:T(8,128)(2,1)S(1)}, u32[]{:S(2)}, u32[]{:S(2)}) async-start(bf16[32,8,512]{2,0,1:T(8,128)(2,1)} %bitcast.136), calls=%async_computation.1 | async-start | bytes 524288 | tf_op jit(solution)/shard_map/all_to_all | solution.py:42
  40.6 13.7 %all-to-all-start.2 = ((bf16[32,8,512]{2,0,1:T(8,128)(2,1)}), bf16[32,8,512]{2,0,1:T(8,128)(2,1)S(1)}, u32[]{:S(2)}, u32[]{:S(2)}) async-start(bf16[32,8,512]{2,0,1:T(8,128)(2,1)} %bitcast.135), calls=%async_computation.2 | async-start | bytes 524288 | tf_op jit(solution)/shard_map/all_to_all | solution.py:43
  54.3 14.2 %all-to-all-start.3 = ((bf16[32,8,512]{2,0,1:T(8,128)(2,1)}), bf16[32,8,512]{2,0,1:T(8,128)(2,1)S(1)}, u32[]{:S(2)}, u32[]{:S(2)}) async-start(bf16[32,8,512]{2,0,1:T(8,128)(2,1)} %bitcast.134), calls=%async_computation.3 | async-start | bytes 524288 | tf_op jit(solution)/shard_map/all_to_all | solution.py:44
  59.5 203.5 %all-reduce.11.cloned.1.call-start = ((), (), s32[]{:S(2)}) async-start(), calls=%async_computation.4 | async-start | bytes 1048576 | tf_op jit(solution)/shard_map/psum | solution.py:13
  69.5 549.0 %all-gather.3.cloned.1.call-start = ((), (), s32[]{:S(2)}) async-start(), calls=%async_computation.5 | async-start | bytes 17039360 | tf_op jit(solution)/shard_map/all_gather | solution.py:120
  69.7 446.6 %copy-start.4 = (bf16[256,4,128]{2,1,0:T(4,128)(2,1)}, bf16[256,4,128]{2,1,0:T(4,128)(2,1)S(1)}, u32[]{:S(2)}) copy-start(bf16[256,4,128]{2,1,0:T(4,128)(2,1)S(1)} %reshape.264) | copy-start | bytes 786436
  264.3 256.5 %copy-start.7 = (bf16[1,128,512]{1,2,0:T(8,128)(2,1)}, bf16[1,128,512]{1,2,0:T(8,128)(2,1)S(1)}, u32[]{:S(2)}) copy-start(bf16[1,128,512]{1,2,0:T(8,128)(2,1)S(1)} %copy.113) | copy-start | bytes 393220
  515.1 362.4 %all-reduce.13.cloned.1.call-start = ((), (), s32[]{:S(2)}) async-start(), calls=%async_computation.6 | async-start | bytes 1048576 | tf_op jit(solution)/shard_map/psum | solution.py:178
  516.2 7.1 collective-permute-start
  518.7 4.7 collective-permute-start.1
  520.8 5.7 copy-start.13
  543.0 9.3 %copy-start.12 = (bf16[2,4,128,512]{2,3,1,0:T(8,128)(2,1)S(1)}, bf16[2,4,128,512]{2,3,1,0:T(8,128)(2,1)}, u32[]{:S(2)}) copy-start(bf16[2,4,128,512]{2,3,1,0:T(8,128)(2,1)} %copy-done.11) | copy-start | bytes 3145732
  543.0 9.3 %copy-start.17 = (bf16[2,128,4,128]{3,1,2,0:T(8,128)(2,1)S(1)}, bf16[2,128,4,128]{3,1,2,0:T(8,128)(2,1)}, u32[]{:S(2)}) copy-start(bf16[2,128,4,128]{3,1,2,0:T(8,128)(2,1)} %copy-done.16) | copy-start | bytes 786436
  543.0 9.3 %copy-start.21 = (bf16[2,128,4,128]{3,1,2,0:T(8,128)(2,1)S(1)}, bf16[2,128,4,128]{3,1,2,0:T(8,128)(2,1)}, u32[]{:S(2)}) copy-start(bf16[2,128,4,128]{3,1,2,0:T(8,128)(2,1)} %copy.124) | copy-start | bytes 786436
  543.0 9.3 %copy-start.23 = (bf16[2,128,4,128]{3,1,2,0:T(8,128)(2,1)S(1)}, bf16[2,128,4,128]{3,1,2,0:T(8,128)(2,1)}, u32[]{:S(2)}) copy-start(bf16[2,128,4,128]{3,1,2,0:T(8,128)(2,1)} %copy-done.22) | copy-start | bytes 786436
  543.0 9.3 %copy-start.26 = (bf16[2,128,4,128]{3,1,2,0:T(8,128)(2,1)S(1)}, bf16[2,128,4,128]{3,1,2,0:T(8,128)(2,1)}, u32[]{:S(2)}) copy-start(bf16[2,128,4,128]{3,1,2,0:T(8,128)(2,1)} %copy-done.25) | copy-start | bytes 786436
  543.9 16.0 %collective-permute-start.2 = (bf16[2,128,4,128]{1,3,2,0:T(8,128)(2,1)}, bf16[2,128,4,128]{1,3,2,0:T(8,128)(2,1)}, u32[]{:S(2)}, u32[]{:S(2)}) collective-permute-start(bf16[2,128,4,128]{1,3,2,0:T(8,128)(2,1)} %fusion.28), channel_id=1, source_target_pairs={{0,8},{8,16},{16,24},{24,32},{32,40},{40,48},{48,56},{56,64},{64,7... | collective-permute-start | bytes 786440 | tf_op jit(solution)/shard_map/ppermute | solution.py:36
  550.0 11.9 %collective-permute-start.3 = (bf16[2,128,4,128]{1,3,2,0:T(8,128)(2,1)}, bf16[2,128,4,128]{1,3,2,0:T(8,128)(2,1)}, u32[]{:S(2)}, u32[]{:S(2)}) collective-permute-start(bf16[2,128,4,128]{1,3,2,0:T(8,128)(2,1)} %fusion.29), channel_id=1, source_target_pairs={{8,0},{16,8},{24,16},{32,24},{40,32},{48,40},{56,48},{64,56},{72,6... | collective-permute-start | bytes 786440 | tf_op jit(solution)/shard_map/ppermute | solution.py:36
  618.5 7.5 copy-start.5
  626.3 248.3 %copy-start.10 = (bf16[128,4,128]{0,2,1:T(8,128)(2,1)S(1)}, bf16[128,4,128]{0,2,1:T(8,128)(2,1)}, u32[]{:S(2)}) copy-start(bf16[128,4,128]{0,2,1:T(8,128)(2,1)} %copy-done.9) | copy-start | bytes 393220
  626.3 251.1 %copy-start.6 = (f32[1,256,4,128]{1,3,2,0:T(8,128)S(1)}, f32[1,256,4,128]{1,3,2,0:T(8,128)}, u32[]{:S(2)}) copy-start(f32[1,256,4,128]{1,3,2,0:T(8,128)} %convolution_bitcast_fusion) | copy-start | bytes 1572868
  (17 other events, 37.0 us)
Sparse Core Ops, SparseCore 0:
  69.6 193.3 all-reduce.10
  515.3 103.1 all-gather.2
  622.0 190.6 all-reduce.12
